TPU v7x, 32 devices: a whole 2x2x4 slice. The times are simulated.
32 devices in a mesh: seq: 8 (over y, x, core), head: 4 (over z).
Axes of the slice: x: 2, y: 2, z: 4, core: 2. Of those that a mesh axis runs over, the one named last changes fastest.
Arguments:
- queries: bfloat16 [2048, 64, 128], P('seq', 'head'), may hold values from -200 to 200
- keys: bfloat16 [2048, 8, 128], P('seq', 'head'), may hold values from -8 to 8
- values: bfloat16 [2048, 8, 128], P('seq', 'head'), may hold values from -6 to 6
- query_map: bfloat16 [64, 128, 64], P('head'), may hold values from -40 to 40
- key_map: bfloat16 [8, 128, 64], P('head'), may hold values from -40 to 40
Outputs:
- teacher_attn: bfloat16 [2048, 64, 128], P('seq', 'head')
- student_attn: bfloat16 [2048, 64, 128], P('seq', 'head')
- loss: float32 [], replicated
All inputs are finite; a program needn't handle non-finite values.
Results may differ from a plain program's by a relative error of at most 0.01.
Values may be sent and summed in bfloat16 or wider, within the bound.
A program may use at most 320 MiB of HBM per device.

v0:
```python
import jax
import jax.numpy as jnp
from jax import lax
from jax.sharding import PartitionSpec as P


def features(rows, projection):
    mapped = jnp.einsum("thd,hdf->thf", rows, projection, preferred_element_type=jnp.float32)
    both = jnp.concatenate(
        [jax.nn.softmax(mapped, axis=-1), jax.nn.softmax(-mapped, axis=-1)], axis=-1
    )
    return both.astype(jnp.bfloat16)


def make_update(query_block, query_pos, key_part, value_part, scale):
    key_pos = jnp.arange(key_part.shape[0], dtype=jnp.int32)
    allowed = query_pos[:, None] >= key_pos[None, :]

    def update(carry):
        top, total, mixed = carry
        scores = (
            jnp.einsum("qgsd,kgd->gsqk", query_block, key_part, preferred_element_type=jnp.float32)
            * scale
        )
        scores = jnp.where(allowed[None, None], scores, -1e30)
        new_top = jnp.maximum(top, jnp.max(scores, axis=-1))
        weight = jnp.where(allowed[None, None], jnp.exp(scores - new_top[..., None]), 0.0)
        total = jnp.sum(weight, axis=-1)
        added = jnp.einsum(
            "gsqk,kgd->qgsd",
            weight.astype(jnp.bfloat16),
            value_part,
            preferred_element_type=jnp.float32,
        )
        mixed = added
        return (new_top, total, mixed)

    return update


def local(queries, keys, values, query_map, key_map):
    rows, heads, head_size = queries.shape
    kv_heads = keys.shape[1]
    group = heads // kv_heads
    seq_count = lax.axis_size("seq")
    position = lax.axis_index("seq")
    scale = 1.0 / head_size**0.5
    grouped = queries.reshape(rows, kv_heads, group, head_size)
    own_first = position * rows
    blocks = [(grouped, own_first + jnp.arange(rows, dtype=jnp.int32))]
    initial = tuple(
        (
            (
                jnp.full((kv_heads, group, block.shape[0]), -1e30, jnp.float32),
                jnp.zeros((kv_heads, group, block.shape[0]), jnp.float32),
                jnp.zeros((block.shape[0], kv_heads, group, head_size), jnp.float32),
            )
            for block, block_pos in blocks
        )
    )
    key_part = lax.all_gather(keys, "seq", axis=0, tiled=True)
    value_part = lax.all_gather(values, "seq", axis=0, tiled=True)
    index = 0
    block, block_pos = blocks[index]
    update = make_update(block, block_pos, key_part, value_part, scale)
    needed = jnp.int32(0) <= jnp.max(block_pos)
    results = [lax.cond(needed, update, lambda kept: kept, initial[index])]
    finals = tuple(results)
    index = 0
    top, total, mixed = finals[index]
    done = mixed / total.transpose(2, 0, 1)[..., None]
    outputs = done.reshape(done.shape[0], heads, head_size).astype(jnp.bfloat16)
    phi_q = features(queries, query_map).reshape(rows, kv_heads, group, -1)
    phi_k = features(keys, key_map)
    lower = jnp.tril(jnp.ones((rows, rows), dtype=bool))
    inner = jnp.einsum("cgsf,egf->gsce", phi_q, phi_k, preferred_element_type=jnp.float32)
    inner = jnp.where(lower[None, None], inner, 0.0)
    den_local = jnp.sum(inner, axis=-1)
    num_local = jnp.einsum(
        "gsce,egd->cgsd", inner.astype(jnp.bfloat16), values, preferred_element_type=jnp.float32
    )
    state_local = jnp.einsum("cgf,cgd->gfd", phi_k, values, preferred_element_type=jnp.float32)
    norm_local = jnp.sum(phi_k.astype(jnp.float32), axis=0)
    state_piece = lax.all_gather(
        state_local[None].astype(jnp.bfloat16), "seq", axis=0, tiled=True
    ).astype(jnp.float32)
    norm_piece = lax.all_gather(
        norm_local[None].astype(jnp.bfloat16), "seq", axis=0, tiled=True
    ).astype(jnp.float32)
    earlier = (jnp.arange(state_piece.shape[0], dtype=jnp.int32) < position).astype(jnp.float32)
    state_prev = jnp.zeros_like(state_local) + jnp.einsum(
        "n,ngfd->gfd", earlier, state_piece, precision=lax.Precision.HIGHEST
    )
    norm_prev = jnp.zeros_like(norm_local) + jnp.einsum(
        "n,ngf->gf", earlier, norm_piece, precision=lax.Precision.HIGHEST
    )
    num_prev = jnp.einsum(
        "cgsf,gfd->cgsd", phi_q, state_prev.astype(jnp.bfloat16), preferred_element_type=jnp.float32
    )
    phi_wide = phi_q.astype(jnp.float32)
    den_prev = jnp.einsum("cgsf,gf->gsc", phi_wide, norm_prev, precision=lax.Precision.HIGHEST)
    denom = (den_local + den_prev).transpose(2, 0, 1)[..., None]
    student_attn = (
        ((num_local + num_prev) / denom).astype(jnp.bfloat16).reshape(rows, heads, head_size)
    )
    diff = outputs.astype(jnp.float32) - student_attn.astype(jnp.float32)
    total_sq = lax.psum(jnp.sum(diff * diff), ("seq", "head"))
    loss = total_sq / (rows * seq_count * heads * lax.axis_size("head") * head_size)
    return (outputs, student_attn, loss)


def solution(mesh):
    placed = (
        P("seq", "head", None),
        P("seq", "head", None),
        P("seq", "head", None),
        P("head", None, None),
        P("head", None, None),
    )
    return jax.shard_map(
        local,
        mesh=mesh,
        in_specs=placed,
        out_specs=(P("seq", "head", None), P("seq", "head", None), P()),
        check_vma=False,
    )
```

profile of v0, /device:TPU:0, one launch (start us, length us, event | category | flops | bytes accessed | tf_op | source)
XLA Modules:
  0.0 166.8 jit_solution(18436730985664525959)
XLA Ops:
  7.2 0.0 copy-start
  7.2 0.0 all-gather.6.cloned.1.call-start
  7.2 1.6 copy.24
  8.8 0.0 all-gather.6.cloned.1.call-update
  8.9 0.0 all-gather.8.cloned.1.call-start
  8.9 1.6 copy.25
  10.5 0.0 all-gather.8.cloned.1.call-update
  10.5 1.1 fusion.71
  11.6 1.1 fusion.72
  12.8 0.0 copy-done
  12.8 0.0 copy-start.2
  12.8 2.0 %fusion.35 = bf16[256,16,64]{0,2,1:T(8,128)(2,1)S(1)} fusion(bf16[16,128,64]{1,2,0:T(8,128)(2,1)S(1)} %copy-done, bf16[256,16,128]{2,1,0:T(8,128)(2,1)} %param.7), kind=kOutput, calls=%fused_computation.41 | convolution fusion | flops 68165760 | bytes 1835008 | tf_op jit(solution)/shard_map/div | solution.py:10
  14.8 0.0 copy-done.2
  14.8 0.6 fusion.36
  15.4 0.0 copy-start.6
  15.5 0.0 copy-start.7
  15.5 0.6 copy-done.6
  16.1 0.1 fusion.53
  16.2 0.0 copy-done.7
  16.2 10.3 %all-gather.2 = bf16[8,2,128]{2,1,0:T(2,128)(2,1)S(1)} all-gather(bf16[1,2,128]{2,1,0:T(2,128)(2,1)S(1)} %bitcast.129), channel_id=3, replica_groups=mesh['seq'=8,'head'=4] {'seq'}, dimensions={0}, use_global_device_ids=true | all-gather | bytes 4608 | tf_op jit(solution)/shard_map/all_gather | solution.py:87
  26.5 0.1 convolution_bitcast_fusion.2
  26.6 0.6 add_reduce_fusion
  27.9 0.5 copy.30
  28.4 1.3 copy.29
  29.7 2.5 %fusion.70 = f32[2,1,256,8]{1,2,3,0:T(8,128)S(1)} fusion(f32[2,128,1,1]{1,2,3,0:T(1,128)S(1)} %convolution_bitcast_fusion.2, bf16[256,2,8,64]{3,0,2,1:T(8,128)(2,1)S(1)} %copy.30, bf16[256,2,8,64]{3,0,2,1:T(8,128)(2,1)} %copy.29), kind=kOutput, calls=%fused_computation.86 | convolution fusion | flops 8388608 | bytes 1065984 | tf_op jit(solution)/shard_map/cgsf,gf->gsc/dot_general | solution.py:101
  32.1 0.0 copy-start.5
  32.1 0.6 copy.52
  32.8 0.3 copy-done.5
  33.0 1.0 convolution_convert_fusion
  34.1 10.0 %all-gather = bf16[16,128,128]{2,1,0:T(8,128)(2,1)S(1)} all-gather(bf16[2,128,128]{2,1,0:T(8,128)(2,1)S(1)} %convolution_convert_fusion), channel_id=2, replica_groups=mesh['seq'=8,'head'=4] {'seq'}, dimensions={0}, use_global_device_ids=true | all-gather | bytes 589824 | tf_op jit(solution)/shard_map/all_gather | solution.py:84
  44.1 0.4 fusion.43
  44.5 0.1 copy.46
  44.7 2.6 %fusion.21 = (f32[2,8,256]{2,1,0:T(8,128)S(1)}, bf16[2,256,256,8]{2,1,3,0:T(8,128)(2,1)S(1)}) fusion(pred[256,256]{0,1:T(8,128)(4,1)S(1)} %iota_compare_fusion, bf16[256,2,8,64]{3,0,2,1:T(8,128)(2,1)S(1)} %copy.30, bf16[256,2,8,64]{3,0,2,1:T(8,128)(2,1)} %copy.29, bf16[256,2,64]{0,2,1:T(8,128)(2,1)} %copy-done.6, bf16[256,2,64]{0,2,1:T(8,128)(2,1)} %copy-done.7), kind=kOutput, calls=%fused_computation.24 | convolution fusion | flops 273936384 | bytes 3358720 | tf_op jit(solution)/shard_map/cgsf,egf->gsce/dot_general | solution.py:76
  47.2 2.3 %fusion.23 = f32[2,8,256,128]{3,2,1,0:T(8,128)} fusion(bf16[2,256,256,8]{2,1,3,0:T(8,128)(2,1)S(1)} %get-tuple-element.58, pred[256,256]{0,1:T(8,128)(4,1)S(1)} %iota_compare_fusion, bf16[256,2,128,1]{2,1,0,3:T(2,128)(2,1)S(1)} %bitcast.126), kind=kOutput, calls=%fused_computation.26 | convolution fusion | flops 269484032 | bytes 4390912 | tf_op jit(solution)/shard_map/gsce,egd->cgsd/dot_general | solution.py:79
  49.6 0.0 all-gather.6.cloned.1.call-done
  49.6 12.4 %all-gather.8.cloned.1.call-done = bf16[2048,2,128]{2,0,1:T(8,128)(2,1)} async-done(((bf16[256,2,128]{2,0,1:T(8,128)(2,1)}), bf16[2048,2,128]{2,0,1:T(8,128)(2,1)}) %all-gather.8.cloned.1.call-update) | async-done | bytes 1048592 | tf_op jit(solution)/shard_map/all_gather | solution.py:62
  61.9 0.0 copy-start.4
  61.9 0.1 ge.26
  62.1 1.1 copy-done.4
  63.1 0.0 copy-start.1
  63.1 47.7 %conditional.1 = (f32[2,8,256]{2,1,0:T(8,128)S(1)}, f32[256,2,8,128]{3,0,2,1:T(8,128)}) conditional(s32[]{:T(128)} %convert_element_type.56, () %tuple.16, (s32[]{:T(128)}, s32[256,1]{0,1:T(1,128)S(1)}, s32[256,2048]{0,1:T(8,128)S(1)}, bf16[256,16,128]{2,1,0:T(8,128)(2,1)}, bf16[2048,2,128]{2,0,1:T(8,128)(2,1)S(1)}, ...), branch_computations={%region_1.0_spmd, %region_2.5_spmd} | conditional | flops 4404539392 | bytes 116493360 | solution.py:67
  63.1 0.0 copy-start.3
  63.1 0.3 broadcast_compare_fusion
  63.4 1.0 copy-done.3
  64.4 0.3 copy.26
  64.7 13.3 %fusion = (f32[2,8,256]{2,1,0:T(8,128)S(1)}, f32[2,2048,256,8]{2,1,3,0:T(8,128)}) fusion(pred[256,2048]{0,1:T(8,128)(4,1)S(1)} %broadcast_compare_fusion, bf16[256,2,8,128]{3,0,2,1:T(8,128)(2,1)S(1)} %bitcast.120, bf16[2048,2,128]{2,0,1:T(8,128)(2,1)S(1)} %get-tuple-element.21), kind=kOutput, calls=%fused_computation.2 | convolution fusion | flops 2172645376 | bytes 36192256 | tf_op jit(solution)/shard_map/cond/branch_1_fun/qgsd,kgd->gsqk/dot_general | solution.py:22
  78.0 14.8 %fusion.2 = f32[2,8,256]{2,1,0:T(8,128)S(1)} fusion(f32[2,2048,256,8]{2,1,3,0:T(8,128)} %get-tuple-element.52, f32[2,8,256]{2,1,0:T(8,128)S(1)} %broadcast_maximum_fusion, pred[256,2048]{0,1:T(8,128)(4,1)S(1)} %broadcast_compare_fusion), kind=kLoop, calls=%fused_computation.4 | loop fusion | flops 41938944 | bytes 34111488 | tf_op jit(solution)/shard_map/cond/branch_1_fun/reduce_sum | solution.py:28
  92.9 17.9 %fusion.6 = f32[256,2,8,128]{3,0,2,1:T(8,128)} fusion(f32[2,2048,256,8]{2,1,3,0:T(8,128)} %get-tuple-element.52, f32[2,8,256]{2,1,0:T(8,128)S(1)} %broadcast_maximum_fusion, pred[256,2048]{0,1:T(8,128)(4,1)S(1)} %broadcast_compare_fusion, bf16[2048,2,128]{2,0,1:T(8,128)(2,1)} %get-tuple-element.23), kind=kOutput, calls=%fused_computation.7 | convolution fusion | flops 2189426688 | bytes 37240832 | tf_op jit(solution)/shard_map/cond/branch_1_fun/gsqk,kgd->qgsd/dot_general | solution.py:29
  110.8 0.0 copy-done.1
  110.8 4.5 %multiply_reduce_fusion = (f32[]{:T(128)}, bf16[256,2,8,128]{3,0,2,1:T(8,128)(2,1)S(1)}, bf16[256,2,8,128]{3,0,2,1:T(8,128)(2,1)S(1)}) fusion(f32[256,2,8,128]{3,0,2,1:T(8,128)} %get-tuple-element.29, f32[256,2,8]{0,2,1:T(8,128)S(1)} %bitcast.127, f32[256,2,8]{0,2,1:T(8,128)S(1)} %bitcast_add_fusion.1, bf16[256,2,8,64]{3,0,2,1:T(8,128)(2,1)S(1)} %copy.30, ...), kind=kOutput, calls=%fused_computation.30 | convolution fusion | flops 141557760 | bytes 7438340 | tf_op jit(solution)/shard_map/cgsf,gfd->cgsd/dot_general | solution.py:97
  115.4 1.6 copy.36
  117.0 1.6 copy.37
  118.7 39.5 %psum.7 = f32[]{:T(128)} all-reduce(f32[]{:T(128)} %get-tuple-element.49), channel_id=1, replica_groups=mesh['seq'=8,'head'=4] {'seq','head'}, use_global_device_ids=true, to_apply=%region_16.17 | all-reduce | flops 1 | bytes 8 | tf_op jit(solution)/shard_map/psum | solution.py:107
  (6 shorter events, 0.1 us)
Async XLA Ops:
  7.2 5.6 %copy-start = (bf16[16,128,64]{1,2,0:T(8,128)(2,1)S(1)}, bf16[16,128,64]{1,2,0:T(8,128)(2,1)}, u32[]{:S(2)}) copy-start(bf16[16,128,64]{1,2,0:T(8,128)(2,1)} %param.10) | copy-start | bytes 786436
  7.2 42.4 %all-gather.6.cloned.1.call-start = ((), (), s32[]{:S(2)}) async-start(), calls=%async_computation | async-start | bytes 1179648 | tf_op jit(solution)/shard_map/all_gather | solution.py:61
  8.9 53.0 %all-gather.8.cloned.1.call-start = ((), (), s32[]{:S(2)}) async-start(), calls=%async_computation.1 | async-start | bytes 1179648 | tf_op jit(solution)/shard_map/all_gather | solution.py:62
  12.8 2.0 %copy-start.2 = (bf16[256,16,128]{2,1,0:T(8,128)(2,1)S(1)}, bf16[256,16,128]{2,1,0:T(8,128)(2,1)}, u32[]{:S(2)}) copy-start(bf16[256,16,128]{2,1,0:T(8,128)(2,1)} %param.7) | copy-start | bytes 3145732
  15.4 0.6 copy-start.6
  15.5 0.7 copy-start.7
  32.1 0.9 copy-start.5
  61.9 1.2 copy-start.4
  63.1 47.7 %copy-start.1 = (bf16[256,2,8,64]{3,0,2,1:T(8,128)(2,1)S(1)}, bf16[256,2,8,64]{3,0,2,1:T(8,128)(2,1)}, u32[]{:S(2)}) copy-start(bf16[256,2,8,64]{3,0,2,1:T(8,128)(2,1)} %copy.29) | copy-start | bytes 1572868
  63.1 1.3 copy-start.3
Sparse Core Ops, SparseCore 0:
  10.5 26.0 all-gather.5
  38.5 23.3 all-gather.7
where the time goes:
time: 167 us
  blocking collectives  59.7 us (36%)
  matrix products  49.5 us (30%)
  between operations  16.6 us (10%)
  other arithmetic  15.9 us (10%)
  local copies, waits for them, and re-layouts  12.4 us (7%)
  waiting for transfers between devices  12.4 us (7%)
    psum x1, blocking collectives, local(): total_sq = lax.psum(jnp.sum(diff * diff), ('seq', 'head'))  39.5 us
    dot_general x1, matrix products, update(): jnp.einsum('gsqk,kgd->qgsd', weight.astype(jnp.bfloat16), value_part, pre...  17.9 us
    reduce_sum x1, other arithmetic, update(): total = jnp.sum(weight, axis=-1)  14.8 us
    dot_general x1, matrix products, update(): jnp.einsum('qgsd,kgd->gsqk', query_block, key_part, preferred_element_typ...  13.3 us
    all_gather x1, waiting for transfers between devices, local(): value_part = lax.all_gather(values, 'seq', axis=0, tiled=True)  12.4 us
    all_gather x1, blocking collectives, local(): lax.all_gather(norm_local[None].astype(jnp.bfloat16), 'seq', axis=0, tile...  10.3 us
    all_gather x1, blocking collectives, local(): lax.all_gather(state_local[None].astype(jnp.bfloat16), 'seq', axis=0, til...  9.99 us
    unnamed x18, local copies, waits for them, and re-layouts  8.46 us
  transfers between devices with their start and end apart: 2, of which 1 were waited for; matrix products, arithmetic and copies ran while one was open for 11% of the time, Pallas kernels for 0%

commit v1 on v0

v1 whole, which is shorter than its diff:
```python
import functools
import math

import jax
import jax.numpy as jnp
from jax import lax
from jax.experimental import pallas as pl
from jax.experimental.pallas import tpu as pltpu
from jax.sharding import PartitionSpec as P

MESH = pl.DeviceIdType.MESH
NT = (((1,), (1,)), ((), ()))
NN = (((1,), (0,)), ((), ()))
LOW = -1e30


def mm(a, b, dims=NN):
    return lax.dot_general(a, b, dims, preferred_element_type=jnp.float32)


def kernel(
    n,
    m,
    count,
    q_ref,
    kv_ref,
    qm_ref,
    km_ref,
    t_ref,
    s_ref,
    loss_ref,
    kvbuf,
    wide,
    qh,
    phiq,
    top,
    acc,
    sacc,
    state,
    kmt,
    slots1,
    slots2,
    send_sem,
    fwd_sem,
    recv_sem,
    l1_send,
    l1_recv,
    l2_send,
    l2_recv,
):
    rows, heads, d = q_ref.shape
    kvh = kv_ref.shape[0] // 2
    group = heads // kvh
    f = qm_ref.shape[2]
    c2 = math.log2(math.e) / math.sqrt(d)
    p = lax.axis_index("seq")
    hid = lax.axis_index("head")
    chip = p // 2
    core = p % 2
    partner = p + 1 - 2 * core
    chips = n // 2

    barrier = pltpu.get_barrier_semaphore()
    for off in range(1, n):
        pl.semaphore_signal(
            barrier, inc=1, device_id={"seq": lax.rem(p + off, n)}, device_id_type=MESH
        )
    for off in range(1, m):
        pl.semaphore_signal(
            barrier, inc=1, device_id={"head": lax.rem(hid + off, m)}, device_id_type=MESH
        )

    wide[...] = q_ref[...].astype(jnp.float32).reshape(rows * heads, d)
    for h in range(heads):
        qh[h] = wide[pl.ds(h, rows, stride=heads), :].astype(jnp.bfloat16)
    for g in range(kvh):
        km = km_ref[g].astype(jnp.float32)
        kmt[g] = jnp.concatenate([km, -km], axis=1).T.astype(jnp.bfloat16)

    pl.semaphore_wait(barrier, n - 1 + m - 1)

    def direct(to_chip):
        return pltpu.make_async_remote_copy(
            src_ref=kv_ref,
            dst_ref=kvbuf.at[p],
            send_sem=send_sem.at[to_chip],
            recv_sem=recv_sem.at[p],
            device_id={"seq": to_chip * 2 + core},
            device_id_type=MESH,
        )

    def to_partner():
        return pltpu.make_async_remote_copy(
            src_ref=kv_ref,
            dst_ref=kvbuf.at[p],
            send_sem=send_sem.at[chip],
            recv_sem=recv_sem.at[p],
            device_id={"seq": partner},
            device_id_type=MESH,
        )

    def forward(from_chip):
        block = from_chip * 2 + core
        return pltpu.make_async_remote_copy(
            src_ref=kvbuf.at[block],
            dst_ref=kvbuf.at[block],
            send_sem=fwd_sem.at[from_chip],
            recv_sem=recv_sem.at[block],
            device_id={"seq": partner},
            device_id_type=MESH,
        )

    def arrived(block):
        pltpu.make_async_remote_copy(
            src_ref=kvbuf.at[block],
            dst_ref=kvbuf.at[block],
            send_sem=fwd_sem.at[0],
            recv_sem=recv_sem.at[block],
            device_id={"seq": partner},
            device_id_type=MESH,
        ).wait_recv()

    def each_later(act):
        def body(i, carry):
            act(direct(i))
            return carry

        lax.fori_loop(chip + 1, chips, body, 0)

    each_later(lambda copy: copy.start())

    @pl.when(core == 0)
    def _():
        to_partner().start()

    ones = jnp.ones((rows, d), jnp.bfloat16)

    def key_features(k, g):
        u = mm(kmt[g], k, NT)
        parts = []
        for half in (u[:f], u[f:]):
            e = jnp.exp(half - jnp.max(half, axis=0, keepdims=True))
            parts.append(e / jnp.sum(e, axis=0, keepdims=True))
        return jnp.concatenate(parts, axis=0).astype(jnp.bfloat16)

    lower = lax.broadcasted_iota(jnp.int32, (rows, rows), 0) >= lax.broadcasted_iota(
        jnp.int32, (rows, rows), 1
    )
    left = lax.broadcasted_iota(jnp.int32, (rows, 2 * f), 1) < f
    for g in range(kvh):
        k = kv_ref[g]
        v1 = jnp.concatenate([kv_ref[kvh + g], ones], axis=1)
        phik = key_features(k, g)
        state[g] = jnp.zeros_like(state[g])
        for h in range(g * group, (g + 1) * group):
            q = qh[h]
            s = jnp.where(lower, mm(q, k, NT), LOW)
            high = jnp.max(s, axis=1, keepdims=True)
            w = jnp.exp2((s - high) * c2).astype(jnp.bfloat16)
            top[h] = jnp.broadcast_to(high, (rows, d))
            acc[h] = mm(w, v1)
            qm = qm_ref[h]
            u = mm(q, jnp.concatenate([qm, -qm], axis=1))
            m1 = jnp.max(jnp.where(left, u, -jnp.inf), axis=1, keepdims=True)
            m2 = jnp.max(jnp.where(left, -jnp.inf, u), axis=1, keepdims=True)
            e = jnp.exp(u - jnp.where(left, m1, m2))
            z1 = jnp.sum(jnp.where(left, e, 0.0), axis=1, keepdims=True)
            z2 = jnp.sum(jnp.where(left, 0.0, e), axis=1, keepdims=True)
            phi = (e / jnp.where(left, z1, z2)).astype(jnp.bfloat16)
            phiq[h] = phi
            a = jnp.where(lower, mm(phi, phik), 0.0).astype(jnp.bfloat16)
            sacc[h] = mm(a, v1)

    def step(blocks):
        for g in range(kvh):
            k = jnp.concatenate([kvbuf[b, g] for b in blocks], axis=0)
            v = jnp.concatenate([kvbuf[b, kvh + g] for b in blocks], axis=0)
            v1 = jnp.concatenate([v, jnp.ones_like(v)], axis=1)
            state[g] += mm(key_features(k, g), v1)
            for h in range(g * group, (g + 1) * group):
                s = mm(qh[h], k, NT)
                before = top[h]
                high = jnp.maximum(before, jnp.max(s, axis=1, keepdims=True))
                top[h] = high
                w = jnp.exp2((s - jnp.concatenate([high] * (s.shape[1] // d), axis=1)) * c2)
                fade = jnp.exp2((before - high) * c2)
                acc[h] = acc[h] * jnp.concatenate([fade, fade], axis=1) + mm(
                    w.astype(jnp.bfloat16), v1
                )

    @pl.when(core == 1)
    def _():
        arrived(p - 1)
        step([p - 1])

    def chip_step(i, carry):
        other = chip - 1 - i
        arrived(other * 2 + core)
        forward(other).start()
        arrived(other * 2 + 1 - core)
        step([other * 2, other * 2 + 1])
        return carry

    lax.fori_loop(0, chip, chip_step, 0)

    part = jnp.zeros((8, d), jnp.float32)
    for h in range(heads):
        a = acc[h]
        wide[pl.ds(h, rows, stride=heads), :] = a[:, :d] / a[:, d:]
    teacher = wide[...].astype(jnp.bfloat16)
    t_ref[...] = teacher.reshape(rows, heads, d)
    for h in range(heads):
        st = state[h // group].astype(jnp.bfloat16)
        a = sacc[h] + mm(phiq[h], st)
        wide[pl.ds(h, rows, stride=heads), :] = a[:, :d] / a[:, d:]
    student = wide[...].astype(jnp.bfloat16)
    s_ref[...] = student.reshape(rows, heads, d)
    diff = t_ref[...].astype(jnp.float32) - s_ref[...].astype(jnp.float32)
    part = jnp.sum((diff * diff).reshape(rows * heads // 8, 8, d), axis=0)

    def exchange(slots, me, size, axis, send, recv, value):
        slots[me] = value

        def copy(off):
            return pltpu.make_async_remote_copy(
                src_ref=slots.at[me],
                dst_ref=slots.at[me],
                send_sem=send.at[off],
                recv_sem=recv.at[off],
                device_id={axis: lax.rem(me + off, size)},
                device_id_type=MESH,
            )

        def landed(off):
            src = lax.rem(me + size - off, size)
            pltpu.make_async_remote_copy(
                src_ref=slots.at[src],
                dst_ref=slots.at[src],
                send_sem=send.at[off],
                recv_sem=recv.at[off],
                device_id={axis: lax.rem(me + off, size)},
                device_id_type=MESH,
            ).wait_recv()

        for off in range(1, size):
            copy(off).start()
        for off in range(1, size):
            landed(off)
        total = slots[0]
        for j in range(1, size):
            total = total + slots[j]
        return total, lambda: [copy(off).wait_send() for off in range(1, size)]

    total, end1 = exchange(slots1, p, n, "seq", l1_send, l1_recv, part)
    total, end2 = exchange(slots2, hid, m, "head", l2_send, l2_recv, total)
    loss_ref[0, 0] = jnp.sum(total) * (1.0 / count)

    end1()
    end2()
    each_later(lambda copy: copy.wait_send())

    @pl.when(core == 0)
    def _():
        to_partner().wait_send()

    def sent(i, carry):
        forward(chip - 1 - i).wait_send()
        return carry

    lax.fori_loop(0, chip, sent, 0)


def local(queries, keys, values, query_map, key_map):
    rows, heads, d = queries.shape
    kvh = keys.shape[1]
    n, m = lax.axis_size("seq"), lax.axis_size("head")
    f = query_map.shape[2]
    count = rows * n * heads * m * d
    kv = jnp.concatenate([keys.transpose(1, 0, 2), values.transpose(1, 0, 2)], axis=0)
    vmem = pl.BlockSpec(memory_space=pltpu.VMEM)
    dma = pltpu.SemaphoreType.DMA
    t, s, loss = pl.pallas_call(
        functools.partial(kernel, n, m, count),
        out_shape=(
            jax.ShapeDtypeStruct(queries.shape, jnp.bfloat16),
            jax.ShapeDtypeStruct(queries.shape, jnp.bfloat16),
            jax.ShapeDtypeStruct((1, 1), jnp.float32),
        ),
        in_specs=[vmem] * 4,
        out_specs=(vmem, vmem, pl.BlockSpec(memory_space=pltpu.SMEM)),
        scratch_shapes=[
            pltpu.VMEM((n, 2 * kvh, rows, d), jnp.bfloat16),
            pltpu.VMEM((rows * heads, d), jnp.float32),
            pltpu.VMEM((heads, rows, d), jnp.bfloat16),
            pltpu.VMEM((heads, rows, 2 * f), jnp.bfloat16),
            pltpu.VMEM((heads, rows, d), jnp.float32),
            pltpu.VMEM((heads, rows, 2 * d), jnp.float32),
            pltpu.VMEM((heads, rows, 2 * d), jnp.float32),
            pltpu.VMEM((kvh, 2 * f, 2 * d), jnp.float32),
            pltpu.VMEM((kvh, 2 * f, d), jnp.bfloat16),
            pltpu.VMEM((n, 8, d), jnp.float32),
            pltpu.VMEM((m, 8, d), jnp.float32),
            dma((n // 2,)),
            dma((n // 2,)),
            dma((n,)),
            dma((n,)),
            dma((n,)),
            dma((m,)),
            dma((m,)),
        ],
        compiler_params=pltpu.CompilerParams(
            collective_id=0, has_side_effects=True, vmem_limit_bytes=60 * 2**20
        ),
    )(queries, kv, query_map, key_map)
    return t, s, loss.reshape(())


def solution(mesh):
    placed = (
        P("seq", "head", None),
        P("seq", "head", None),
        P("seq", "head", None),
        P("head", None, None),
        P("head", None, None),
    )
    return jax.shard_map(
        local,
        mesh=mesh,
        in_specs=placed,
        out_specs=(P("seq", "head", None), P("seq", "head", None), P()),
        check_vma=False,
    )
```

time: 167 us -> 51.2 us (0.31)
  blocking collectives: 59.7 us -> 0 us
  matrix products: 49.5 us -> 0 us
  Pallas kernels: 0 us -> 40.5 us
  other arithmetic: 15.9 us -> 0.73 us
  between operations: 16.6 us -> 2.47 us
  waiting for transfers between devices: 12.4 us -> 0 us
  local copies, waits for them, and re-layouts: 12.4 us -> 7.21 us
    dot_general x9 -> x0, matrix products: 44.7 us -> none  [the longest x1 17.9 us: update(): jnp.einsum('gsqk,kgd->qgsd', weight.astype(jnp.bfloat16), value_part, pre...]
    pallas_call x0 -> x1, Pallas kernels: none -> 40.5 us  [local(): pl.pallas_call(functools.partial(kernel, n, m, count), out_shape=(jax.Sha...]
    psum x1 -> x0, blocking collectives: 39.5 us -> none  [local(): total_sq = lax.psum(jnp.sum(diff * diff), ('seq', 'head'))]
    all_gather x2 -> x0, blocking collectives: 20.3 us -> none  [the longest x1 10.3 us: local(): lax.all_gather(norm_local[None].astype(jnp.bfloat16), 'seq', axis=0, tile...]
    reduce_sum x2 -> x0, other arithmetic: 15 us -> none  [the longest x1 14.8 us: update(): total = jnp.sum(weight, axis=-1)]
    all_gather x2 -> x0, waiting for transfers between devices: 12.4 us -> none  [the longest x1 12.4 us: local(): value_part = lax.all_gather(values, 'seq', axis=0, tiled=True)]
    div x2 -> x0, matrix products: 2.58 us -> none  [the longest x1 1.97 us: features(): jax.nn.softmax(-mapped, axis=-1)]
    sub x2 -> x0, matrix products: 2.29 us -> none  [the longest x1 1.14 us: features(): jax.nn.softmax(-mapped, axis=-1)]
  transfers between devices with their start and end apart: 2 -> 0, of which waited for: 1 -> 0; matrix products, arithmetic and copies ran while one was open for 11% -> 0% of each run, Pallas kernels for 0% -> 0%
where the time goes in v1:
time: 51.2 us; the launch traced here: 50.9 us
  Pallas kernels  40.5 us (79%)
  local copies, waits for them, and re-layouts  7.21 us (14%)
  between operations  2.47 us (5%)
  other arithmetic  0.73 us (1%)
    pallas_call x1, Pallas kernels, local(): pl.pallas_call(functools.partial(kernel, n, m, count), out_shape=(jax.Sha...  40.5 us
    unnamed x8, local copies, waits for them, and re-layouts  6.21 us

profile of v1, /device:TPU:0, one launch (start us, length us, event | category | flops | bytes accessed | tf_op | source)
XLA Modules:
  0.0 50.9 jit_solution(10657356294283483630)
XLA Ops:
  0.6 1.5 %copy.11.km_ref = bf16[2,128,64]{2,1,0:T(8,128)(2,1)} copy(bf16[2,128,64]{1,2,0:T(8,128)(2,1)} %param.9) | data formatting | bytes 65536 | tf_op args[4]
  2.1 1.0 %copy_bitcast_fusion = (bf16[2,256,128]{2,1,0:T(8,128)(2,1)S(1)}, bf16[2,256,128]{2,1,0:T(8,128)(2,1)S(1)}) fusion(bf16[256,2,128]{2,1,0:T(2,128)(2,1)} %param.7, bf16[256,2,128]{2,1,0:T(2,128)(2,1)} %param.6), kind=kLoop, calls=%fused_computation.1 | loop fusion | bytes 524288 | tf_op jit(solution)/shard_map/transpose | solution.py:279
  3.1 0.0 copy-start.1
  3.1 0.7 %pad_maximum_fusion.kv_ref = bf16[4,256,128]{2,1,0:T(8,128)(2,1)} fusion(bf16[2,256,128]{2,1,0:T(8,128)(2,1)S(1)} %get-tuple-element.9, bf16[2,256,128]{2,1,0:T(8,128)(2,1)S(1)} %get-tuple-element.10), kind=kLoop, calls=%fused_computation | loop fusion | flops 131072 | bytes 524288 | tf_op jit(solution)/shard_map/concatenate | solution.py:279
  3.9 0.3 copy-done.1
  4.1 1.0 %copy.10.qm_ref = bf16[16,128,64]{2,1,0:T(8,128)(2,1)} copy(bf16[16,128,64]{1,2,0:T(8,128)(2,1)S(1)} %copy-done.1) | data formatting | bytes 524288 | tf_op args[3]
  5.1 40.5 %shard_map.76 = (bf16[256,16,128]{2,1,0:T(8,128)(2,1)}, bf16[256,16,128]{2,1,0:T(8,128)(2,1)}, f32[1,1]{1,0:T(1,128)}) custom-call(bf16[256,16,128]{2,1,0:T(8,128)(2,1)} %q_ref.1, bf16[4,256,128]{2,1,0:T(8,128)(2,1)} %pad_maximum_fusion.kv_ref, bf16[16,128,64]{2,1,0:T(8,128)(2,1)} %copy.10.qm_ref, bf16[2,128,64]{2,1,0:T(8,128)(2,1)} %copy.11.km_ref), custom_call_target="tpu_custom_call" | custom-call | tf_op jit(solution)/shard_map/pallas_call | solution.py:282
  45.6 0.0 copy-start
  45.6 2.5 %copy.17 = bf16[256,16,128]{2,1,0:T(8,128)(2,1)} copy(bf16[256,16,128]{2,1,0:T(8,128)(2,1)} %get-tuple-element.14) | data formatting | bytes 2097152
  48.1 0.0 copy-done
  48.1 1.0 %copy.18 = bf16[256,16,128]{2,1,0:T(8,128)(2,1)} copy(bf16[256,16,128]{2,1,0:T(8,128)(2,1)S(1)} %copy-done) | data formatting | bytes 2097152
Async XLA Ops:
  3.1 1.0 %copy-start.1 = (bf16[16,128,64]{1,2,0:T(8,128)(2,1)S(1)}, bf16[16,128,64]{1,2,0:T(8,128)(2,1)}, u32[]{:S(2)}) copy-start(bf16[16,128,64]{1,2,0:T(8,128)(2,1)} %param.8) | copy-start | bytes 786436
  45.6 2.5 %copy-start = (bf16[256,16,128]{2,1,0:T(8,128)(2,1)S(1)}, bf16[256,16,128]{2,1,0:T(8,128)(2,1)}, u32[]{:S(2)}) copy-start(bf16[256,16,128]{2,1,0:T(8,128)(2,1)} %get-tuple-element.15) | copy-start | bytes 3145732

commit v2 on v1

v2 whole, which is shorter than its diff:
```python
import functools
import math

import jax
import jax.numpy as jnp
from jax import lax
from jax.experimental import pallas as pl
from jax.experimental.pallas import tpu as pltpu
from jax.sharding import PartitionSpec as P

MESH = pl.DeviceIdType.MESH
NT = (((1,), (1,)), ((), ()))
NN = (((1,), (0,)), ((), ()))
LOW = -1e30


def mm(a, b, dims=NN):
    return lax.dot_general(a, b, dims, preferred_element_type=jnp.float32)


def kernel(
    n,
    m,
    count,
    q_ref,
    k_ref,
    v_ref,
    qm_ref,
    km_ref,
    t_ref,
    s_ref,
    loss_ref,
    kvbuf,
    wide,
    qh,
    phiq,
    top,
    acc,
    sacc,
    state,
    slots1,
    slots2,
    send_sem,
    fwd_sem,
    recv_sem,
    l1_send,
    l1_recv,
    l2_send,
    l2_recv,
):
    rows, heads, d = q_ref.shape
    kvh = k_ref.shape[0]
    group = heads // kvh
    f = qm_ref.shape[1]
    c2 = math.log2(math.e) / math.sqrt(d)
    p = lax.axis_index("seq")
    hid = lax.axis_index("head")
    chip = p // 2
    core = p % 2
    partner = p + 1 - 2 * core
    chips = n // 2

    barrier = pltpu.get_barrier_semaphore()
    for off in range(1, n):
        pl.semaphore_signal(
            barrier, inc=1, device_id={"seq": lax.rem(p + off, n)}, device_id_type=MESH
        )
    for off in range(1, m):
        pl.semaphore_signal(
            barrier, inc=1, device_id={"head": lax.rem(hid + off, m)}, device_id_type=MESH
        )

    wide[...] = q_ref[...].astype(jnp.float32).reshape(rows * heads, d)
    for h in range(heads):
        qh[h] = wide[pl.ds(h, rows, stride=heads), :].astype(jnp.bfloat16)

    pl.semaphore_wait(barrier, n - 1 + m - 1)

    def own(part, device, sem):
        return pltpu.make_async_remote_copy(
            src_ref=(k_ref, v_ref)[part],
            dst_ref=kvbuf.at[p, part],
            send_sem=send_sem.at[part, sem],
            recv_sem=recv_sem.at[part, p],
            device_id={"seq": device},
            device_id_type=MESH,
        )

    def forward(part, from_chip):
        block = from_chip * 2 + core
        return pltpu.make_async_remote_copy(
            src_ref=kvbuf.at[block, part],
            dst_ref=kvbuf.at[block, part],
            send_sem=fwd_sem.at[part, from_chip],
            recv_sem=recv_sem.at[part, block],
            device_id={"seq": partner},
            device_id_type=MESH,
        )

    def arrived(part, block):
        pltpu.make_async_remote_copy(
            src_ref=kvbuf.at[block, part],
            dst_ref=kvbuf.at[block, part],
            send_sem=fwd_sem.at[part, 0],
            recv_sem=recv_sem.at[part, block],
            device_id={"seq": partner},
            device_id_type=MESH,
        ).wait_recv()

    def each_own(act):
        @pl.when(core == 0)
        def _():
            act(own(0, partner, chip))
            act(own(1, partner, chip))

        def body(i, carry):
            act(own(0, i * 2 + core, i))
            act(own(1, i * 2 + core, i))
            return carry

        lax.fori_loop(chip + 1, chips, body, 0)

    each_own(lambda copy: copy.start())

    ones = jnp.ones((rows, d), jnp.bfloat16)

    def features(x, half_map):
        u = mm(jnp.concatenate([half_map, -half_map], axis=0), x, NT)
        parts = []
        for half in (u[:f], u[f:]):
            e = jnp.exp(half - jnp.max(half, axis=0, keepdims=True))
            parts.append(e * (1.0 / jnp.sum(e, axis=0, keepdims=True)))
        return jnp.concatenate(parts, axis=0)

    def key_features(k, g):
        return features(k, km_ref[g]).astype(jnp.bfloat16)

    lower = lax.broadcasted_iota(jnp.int32, (rows, rows), 0) >= lax.broadcasted_iota(
        jnp.int32, (rows, rows), 1
    )
    for g in range(kvh):
        k = k_ref[g]
        v1 = jnp.concatenate([v_ref[g], ones], axis=1)
        phik = key_features(k, g)
        state[g] = jnp.zeros_like(state[g])
        for h in range(g * group, (g + 1) * group):
            q = qh[h]
            s = jnp.where(lower, mm(q, k, NT), LOW)
            high = jnp.max(s, axis=1, keepdims=True)
            w = jnp.exp2((s - high) * c2).astype(jnp.bfloat16)
            top[h] = jnp.broadcast_to(high, (rows, d))
            acc[h] = mm(w, v1)
            phi = features(q, qm_ref[h]).T.astype(jnp.bfloat16)
            phiq[h] = phi
            a = jnp.where(lower, mm(phi, phik), 0.0).astype(jnp.bfloat16)
            sacc[h] = mm(a, v1)

    def step(blocks):
        for g in range(kvh):
            k = jnp.concatenate([kvbuf[b, 0, g] for b in blocks], axis=0)
            v = jnp.concatenate([kvbuf[b, 1, g] for b in blocks], axis=0)
            v1 = jnp.concatenate([v, jnp.ones_like(v)], axis=1)
            state[g] += mm(key_features(k, g), v1)
            for h in range(g * group, (g + 1) * group):
                s = mm(qh[h], k, NT)
                before = top[h]
                high = jnp.maximum(before, jnp.max(s, axis=1, keepdims=True))
                top[h] = high
                w = jnp.exp2((s - jnp.concatenate([high] * (s.shape[1] // d), axis=1)) * c2)
                fade = jnp.exp2((before - high) * c2)
                acc[h] = acc[h] * jnp.concatenate([fade, fade], axis=1) + mm(
                    w.astype(jnp.bfloat16), v1
                )

    @pl.when(core == 1)
    def _():
        for part in range(2):
            arrived(part, p - 1)
        step([p - 1])

    def chip_step(i, carry):
        other = chip - 1 - i
        for part in range(2):
            arrived(part, other * 2 + core)
            forward(part, other).start()
        for part in range(2):
            arrived(part, other * 2 + 1 - core)
        step([other * 2, other * 2 + 1])
        return carry

    lax.fori_loop(0, chip, chip_step, 0)

    part = jnp.zeros((8, d), jnp.float32)
    for h in range(heads):
        a = acc[h]
        t = (a[:, :d] / a[:, d:]).astype(jnp.bfloat16)
        t_ref[h] = t
        b = sacc[h] + mm(phiq[h], state[h // group].astype(jnp.bfloat16))
        o = (b[:, :d] / b[:, d:]).astype(jnp.bfloat16)
        s_ref[h] = o
        diff = t.astype(jnp.float32) - o.astype(jnp.float32)
        part += jnp.sum((diff * diff).reshape(rows // 8, 8, d), axis=0)

    def exchange(slots, me, size, axis, send, recv, value):
        slots[me] = value

        def copy(off):
            return pltpu.make_async_remote_copy(
                src_ref=slots.at[me],
                dst_ref=slots.at[me],
                send_sem=send.at[off],
                recv_sem=recv.at[off],
                device_id={axis: lax.rem(me + off, size)},
                device_id_type=MESH,
            )

        def landed(off):
            src = lax.rem(me + size - off, size)
            pltpu.make_async_remote_copy(
                src_ref=slots.at[src],
                dst_ref=slots.at[src],
                send_sem=send.at[off],
                recv_sem=recv.at[off],
                device_id={axis: lax.rem(me + off, size)},
                device_id_type=MESH,
            ).wait_recv()

        for off in range(1, size):
            copy(off).start()
        for off in range(1, size):
            landed(off)
        total = slots[0]
        for j in range(1, size):
            total = total + slots[j]
        return total, lambda: [copy(off).wait_send() for off in range(1, size)]

    total, end1 = exchange(slots1, p, n, "seq", l1_send, l1_recv, part)
    total, end2 = exchange(slots2, hid, m, "head", l2_send, l2_recv, total)
    loss_ref[0, 0] = jnp.sum(total) * (1.0 / count)

    end1()
    end2()
    each_own(lambda copy: copy.wait_send())

    def sent(i, carry):
        for part in range(2):
            forward(part, chip - 1 - i).wait_send()
        return carry

    lax.fori_loop(0, chip, sent, 0)


def local(queries, keys, values, query_map, key_map):
    rows, heads, d = queries.shape
    kvh = keys.shape[1]
    n, m = lax.axis_size("seq"), lax.axis_size("head")
    f = query_map.shape[2]
    count = rows * n * heads * m * d
    vmem = pl.BlockSpec(memory_space=pltpu.VMEM)
    dma = pltpu.SemaphoreType.DMA
    t, s, loss = pl.pallas_call(
        functools.partial(kernel, n, m, count),
        out_shape=(
            jax.ShapeDtypeStruct((heads, rows, d), jnp.bfloat16),
            jax.ShapeDtypeStruct((heads, rows, d), jnp.bfloat16),
            jax.ShapeDtypeStruct((1, 1), jnp.float32),
        ),
        in_specs=[vmem] * 5,
        out_specs=(vmem, vmem, pl.BlockSpec(memory_space=pltpu.SMEM)),
        scratch_shapes=[
            pltpu.VMEM((n, 2, kvh, rows, d), jnp.bfloat16),
            pltpu.VMEM((rows * heads, d), jnp.float32),
            pltpu.VMEM((heads, rows, d), jnp.bfloat16),
            pltpu.VMEM((heads, rows, 2 * f), jnp.bfloat16),
            pltpu.VMEM((heads, rows, d), jnp.float32),
            pltpu.VMEM((heads, rows, 2 * d), jnp.float32),
            pltpu.VMEM((heads, rows, 2 * d), jnp.float32),
            pltpu.VMEM((kvh, 2 * f, 2 * d), jnp.float32),
            pltpu.VMEM((n, 8, d), jnp.float32),
            pltpu.VMEM((m, 8, d), jnp.float32),
            dma((2, n // 2)),
            dma((2, n // 2)),
            dma((2, n)),
            dma((n,)),
            dma((n,)),
            dma((m,)),
            dma((m,)),
        ],
        compiler_params=pltpu.CompilerParams(
            collective_id=0, has_side_effects=True, vmem_limit_bytes=60 * 2**20
        ),
    )(
        queries,
        keys.transpose(1, 0, 2),
        values.transpose(1, 0, 2),
        query_map.transpose(0, 2, 1),
        key_map.transpose(0, 2, 1),
    )
    return t.transpose(1, 0, 2), s.transpose(1, 0, 2), loss.reshape(())


def solution(mesh):
    placed = (
        P("seq", "head", None),
        P("seq", "head", None),
        P("seq", "head", None),
        P("head", None, None),
        P("head", None, None),
    )
    return jax.shard_map(
        local,
        mesh=mesh,
        in_specs=placed,
        out_specs=(P("seq", "head", None), P("seq", "head", None), P()),
        check_vma=False,
    )
```

time: 51.2 us -> 46.6 us (0.910)
  Pallas kernels: 40.5 us -> 37.8 us
  local copies, waits for them, and re-layouts: 7.21 us -> 6.32 us
  other arithmetic: 0.73 us -> 0 us
    pallas_call x1, Pallas kernels: 40.5 us -> 37.8 us  [local(): pl.pallas_call(functools.partial(kernel, n, m, count), out_shape=(jax.Sha...]
    unnamed x8 -> x4, local copies, waits for them, and re-layouts: 6.21 us -> 4.61 us
    concatenate x1 -> x0, other arithmetic: 0.73 us -> none  [local(): jnp.concatenate([keys.transpose(1, 0, 2), values.transpose(1, 0, 2)], axi...]
    transpose x1, local copies, waits for them, and re-layouts: 1 us -> 1.7 us  [local(): values.transpose(1, 0, 2)]
where the time goes in v2:
time: 46.6 us; the launch traced here: 46.4 us
  Pallas kernels  37.8 us (81%)
  local copies, waits for them, and re-layouts  6.32 us (14%)
  between operations  2.32 us (5%)
    pallas_call x1, Pallas kernels, local(): pl.pallas_call(functools.partial(kernel, n, m, count), out_shape=(jax.Sha...  37.8 us
    unnamed x4, local copies, waits for them, and re-layouts  4.61 us
    transpose x1, local copies, waits for them, and re-layouts, local(): values.transpose(1, 0, 2)  1.7 us

profile of v2, /device:TPU:0, one launch (start us, length us, event | category | flops | bytes accessed | tf_op | source)
XLA Modules:
  0.0 46.4 jit_solution(11169068189260134419)
XLA Ops:
  0.6 1.7 %copy_bitcast_fusion = (bf16[2,256,128]{2,1,0:T(8,128)(2,1)}, bf16[2,256,128]{2,1,0:T(8,128)(2,1)}) fusion(bf16[256,2,128]{2,1,0:T(2,128)(2,1)} %param.7, bf16[256,2,128]{2,1,0:T(2,128)(2,1)} %param.6), kind=kLoop, calls=%fused_computation | loop fusion | bytes 524288 | tf_op jit(solution)/shard_map/transpose | solution.py:295
  2.3 37.8 %shard_map.76 = (bf16[16,256,128]{2,1,0:T(8,128)(2,1)}, bf16[16,256,128]{2,1,0:T(8,128)(2,1)}, f32[1,1]{1,0:T(1,128)}) custom-call(bf16[256,16,128]{2,1,0:T(8,128)(2,1)} %q_ref.1, bf16[2,256,128]{2,1,0:T(8,128)(2,1)} %get-tuple-element.13.k_ref, bf16[2,256,128]{2,1,0:T(8,128)(2,1)} %get-tuple-element.12.v_ref, bf16[16,64,128]{2,1,0:T(8,128)(2,1)} %bitcast.11, ...), custom_call_target="tpu_custom_call" | custom-call | tf_op jit(solution)/shard_map/pallas_call | solution.py:261
  40.1 0.0 copy-start
  40.1 3.0 %copy.10 = bf16[256,16,128]{2,1,0:T(8,128)(2,1)} copy(bf16[256,16,128]{2,0,1:T(8,128)(2,1)} %bitcast.10) | data formatting | bytes 2097152
  43.1 0.0 copy-done
  43.1 1.6 %copy.11 = bf16[256,16,128]{2,1,0:T(8,128)(2,1)} copy(bf16[256,16,128]{2,0,1:T(8,128)(2,1)S(1)} %bitcast.9) | data formatting | bytes 2097152
Async XLA Ops:
  40.1 3.0 %copy-start = (bf16[16,256,128]{2,1,0:T(8,128)(2,1)S(1)}, bf16[16,256,128]{2,1,0:T(8,128)(2,1)}, u32[]{:S(2)}) copy-start(bf16[16,256,128]{2,1,0:T(8,128)(2,1)} %get-tuple-element.7) | copy-start | bytes 3145732

commit v3 on v2

--- a/solution.py
+++ b/solution.py
@@ -22,7 +22,7 @@
     n,
     m,
     count,
-    q_ref,
+    q_hbm,
     k_ref,
     v_ref,
     qm_ref,
@@ -30,6 +30,7 @@
     t_ref,
     s_ref,
     loss_ref,
+    q_ref,
     kvbuf,
     wide,
     qh,
@@ -42,6 +43,8 @@
     slots2,
     send_sem,
     fwd_sem,
+    relay_sem,
+    local_sem,
     recv_sem,
     l1_send,
     l1_recv,
@@ -49,6 +52,8 @@
     l2_recv,
 ):
     rows, heads, d = q_ref.shape
+    load_q = pltpu.make_async_copy(q_hbm, q_ref, local_sem.at[0])
+    load_q.start()
     kvh = k_ref.shape[0]
     group = heads // kvh
     f = qm_ref.shape[1]
@@ -59,6 +64,7 @@
     core = p % 2
     partner = p + 1 - 2 * core
     chips = n // 2
+    square = chips == 4
 
     barrier = pltpu.get_barrier_semaphore()
     for off in range(1, n):
@@ -70,9 +76,20 @@
             barrier, inc=1, device_id={"head": lax.rem(hid + off, m)}, device_id_type=MESH
         )
 
+    def features(x, half_map):
+        u = mm(jnp.concatenate([half_map, -half_map], axis=0), x, NT)
+        parts = []
+        for half in (u[:f], u[f:]):
+            e = jnp.exp(half - jnp.max(half, axis=0, keepdims=True))
+            parts.append(e * (1.0 / jnp.sum(e, axis=0, keepdims=True)))
+        return jnp.concatenate(parts, axis=0)
+
+    load_q.wait()
     wide[...] = q_ref[...].astype(jnp.float32).reshape(rows * heads, d)
     for h in range(heads):
         qh[h] = wide[pl.ds(h, rows, stride=heads), :].astype(jnp.bfloat16)
+    for h in range(heads):
+        phiq[h] = features(qh[h], qm_ref[h]).T.astype(jnp.bfloat16)
 
     pl.semaphore_wait(barrier, n - 1 + m - 1)
 
@@ -107,12 +124,41 @@
             device_id_type=MESH,
         ).wait_recv()
 
+    def near(to):
+        if to == 0:
+            return (chip == 1) & (core == 0)
+        if to == 3:
+            return (chip == 1) | (chip == 2)
+        return chip == 0
+
+    def relay(part, block, to_chip):
+        return pltpu.make_async_remote_copy(
+            src_ref=kvbuf.at[block, part],
+            dst_ref=kvbuf.at[block, part],
+            send_sem=relay_sem.at[part],
+            recv_sem=recv_sem.at[part, block],
+            device_id={"seq": to_chip * 2 + core},
+            device_id_type=MESH,
+        )
+
+    relays = ((0, 0, 1, 2), (1, 0, 0, 3), (2, 1, 0, 3), (3, 1, 1, 2))
+
     def each_own(act):
         @pl.when(core == 0)
         def _():
             act(own(0, partner, chip))
             act(own(1, partner, chip))
 
+        if square:
+            for to in range(4):
+
+                @pl.when(near(to))
+                def _():
+                    act(own(0, to * 2 + core, to))
+                    act(own(1, to * 2 + core, to))
+
+            return
+
         def body(i, carry):
             act(own(0, i * 2 + core, i))
             act(own(1, i * 2 + core, i))
@@ -123,14 +169,6 @@
     each_own(lambda copy: copy.start())
 
     ones = jnp.ones((rows, d), jnp.bfloat16)
-
-    def features(x, half_map):
-        u = mm(jnp.concatenate([half_map, -half_map], axis=0), x, NT)
-        parts = []
-        for half in (u[:f], u[f:]):
-            e = jnp.exp(half - jnp.max(half, axis=0, keepdims=True))
-            parts.append(e * (1.0 / jnp.sum(e, axis=0, keepdims=True)))
-        return jnp.concatenate(parts, axis=0)
 
     def key_features(k, g):
         return features(k, km_ref[g]).astype(jnp.bfloat16)
@@ -150,9 +188,7 @@
             w = jnp.exp2((s - high) * c2).astype(jnp.bfloat16)
             top[h] = jnp.broadcast_to(high, (rows, d))
             acc[h] = mm(w, v1)
-            phi = features(q, qm_ref[h]).T.astype(jnp.bfloat16)
-            phiq[h] = phi
-            a = jnp.where(lower, mm(phi, phik), 0.0).astype(jnp.bfloat16)
+            a = jnp.where(lower, mm(phiq[h], phik), 0.0).astype(jnp.bfloat16)
             sacc[h] = mm(a, v1)
 
     def step(blocks):
@@ -178,10 +214,32 @@
             arrived(part, p - 1)
         step([p - 1])
 
+    def each_relay(origin, part, act):
+        for who, lane, source, to in relays:
+
+            @pl.when((chip == who) & (core == lane) & (origin == source))
+            def _():
+                act(relay(part, source * 2 + lane, to))
+
+    if square:
+
+        @pl.when((chip == 0) & (core == 0))
+        def _():
+            for part in range(2):
+                arrived(part, 2)
+                relay(part, 2, 2).start()
+
+    def nth(i):
+        if square:
+            return jnp.where(chip == 3, lax.rem(i + 1, 3), i)
+        return chip - 1 - i
+
     def chip_step(i, carry):
-        other = chip - 1 - i
+        other = nth(i)
         for part in range(2):
             arrived(part, other * 2 + core)
+            if square:
+                each_relay(other, part, lambda copy: copy.start())
             forward(part, other).start()
         for part in range(2):
             arrived(part, other * 2 + 1 - core)
@@ -244,10 +302,17 @@
 
     def sent(i, carry):
         for part in range(2):
-            forward(part, chip - 1 - i).wait_send()
+            forward(part, i).wait_send()
         return carry
 
     lax.fori_loop(0, chip, sent, 0)
+    if square:
+        for who, lane, source, to in relays:
+
+            @pl.when((chip == who) & (core == lane))
+            def _():
+                for part in range(2):
+                    relay(part, source * 2 + lane, to).wait_send()
 
 
 def local(queries, keys, values, query_map, key_map):
@@ -257,17 +322,19 @@
     f = query_map.shape[2]
     count = rows * n * heads * m * d
     vmem = pl.BlockSpec(memory_space=pltpu.VMEM)
+    hbm = pl.BlockSpec(memory_space=pl.ANY)
     dma = pltpu.SemaphoreType.DMA
     t, s, loss = pl.pallas_call(
         functools.partial(kernel, n, m, count),
         out_shape=(
-            jax.ShapeDtypeStruct((heads, rows, d), jnp.bfloat16),
-            jax.ShapeDtypeStruct((heads, rows, d), jnp.bfloat16),
+            pltpu.VMEM((heads, rows, d), jnp.bfloat16),
+            pltpu.VMEM((heads, rows, d), jnp.bfloat16),
             jax.ShapeDtypeStruct((1, 1), jnp.float32),
         ),
-        in_specs=[vmem] * 5,
+        in_specs=[hbm] + [vmem] * 4,
         out_specs=(vmem, vmem, pl.BlockSpec(memory_space=pltpu.SMEM)),
         scratch_shapes=[
+            pltpu.VMEM((rows, heads, d), jnp.bfloat16),
             pltpu.VMEM((n, 2, kvh, rows, d), jnp.bfloat16),
             pltpu.VMEM((rows * heads, d), jnp.float32),
             pltpu.VMEM((heads, rows, d), jnp.bfloat16),
@@ -280,6 +347,8 @@
             pltpu.VMEM((m, 8, d), jnp.float32),
             dma((2, n // 2)),
             dma((2, n // 2)),
+            dma((2,)),
+            dma((1,)),
             dma((2, n)),
             dma((n,)),
             dma((n,)),
@@ -287,7 +356,7 @@
             dma((m,)),
         ],
         compiler_params=pltpu.CompilerParams(
-            collective_id=0, has_side_effects=True, vmem_limit_bytes=60 * 2**20
+            collective_id=0, has_side_effects=True, vmem_limit_bytes=48 * 2**20
         ),
     )(
         queries,

time: 46.6 us -> 43 us (0.923)
  Pallas kernels: 37.8 us -> 34.8 us
  local copies, waits for them, and re-layouts: 6.32 us -> 5.58 us
    pallas_call x1, Pallas kernels: 37.8 us -> 34.8 us  [local(): pl.pallas_call(functools.partial(kernel, n, m, count), out_shape=(pltpu.V...]
    transpose x1, local copies, waits for them, and re-layouts: 1.7 us -> 1.04 us  [local(): values.transpose(1, 0, 2)]
    unnamed x4 -> x8, local copies, waits for them, and re-layouts: 4.61 us -> 4.53 us
where the time goes in v3:
time: 43 us; the launch traced here: 42.8 us
  Pallas kernels  34.8 us (81%)
  local copies, waits for them, and re-layouts  5.58 us (13%)
  between operations  2.42 us (6%)
    pallas_call x1, Pallas kernels, local(): pl.pallas_call(functools.partial(kernel, n, m, count), out_shape=(pltpu.V...  34.8 us
    unnamed x8, local copies, waits for them, and re-layouts  4.53 us
    transpose x1, local copies, waits for them, and re-layouts, local(): values.transpose(1, 0, 2)  1.04 us

profile of v3, /device:TPU:0, one launch (start us, length us, event | category | flops | bytes accessed | tf_op | source)
XLA Modules:
  0.0 42.8 jit_solution(2167027335472380637)
XLA Ops:
  0.6 0.0 copy-start.1
  0.6 0.0 copy-start.2
  0.7 1.0 %copy_bitcast_fusion = (bf16[2,256,128]{2,1,0:T(8,128)(2,1)S(1)}, bf16[2,256,128]{2,1,0:T(8,128)(2,1)S(1)}) fusion(bf16[256,2,128]{2,1,0:T(2,128)(2,1)} %param.7, bf16[256,2,128]{2,1,0:T(2,128)(2,1)} %param.6), kind=kLoop, calls=%fused_computation | loop fusion | bytes 524288 | tf_op jit(solution)/shard_map/transpose | solution.py:364
  1.7 0.0 copy-done.1
  1.7 0.0 copy-done.2
  1.7 0.0 copy-start
  1.7 1.2 %copy-done = bf16[256,16,128]{2,1,0:T(8,128)(2,1)S(1)} copy-done((bf16[256,16,128]{2,1,0:T(8,128)(2,1)S(1)}, bf16[256,16,128]{2,1,0:T(8,128)(2,1)}, u32[]{:S(2)}) %copy-start) | copy-done | bytes 1048600
  2.9 34.8 %shard_map.76 = (bf16[16,256,128]{2,1,0:T(8,128)(2,1)S(1)}, bf16[16,256,128]{2,1,0:T(8,128)(2,1)S(1)}, f32[1,1]{1,0:T(1,128)}) custom-call(bf16[256,16,128]{2,1,0:T(8,128)(2,1)S(1)} %copy-done, bf16[2,256,128]{2,1,0:T(8,128)(2,1)S(1)} %get-tuple-element.13.k_ref, bf16[2,256,128]{2,1,0:T(8,128)(2,1)S(1)} %get-tuple-element.12.v_ref, ...), custom_call_target="tpu_custom_call" | custom-call | tf_op jit(solution)/shard_map/pallas_call | solution.py:327
  37.7 1.6 %copy.10 = bf16[256,16,128]{2,1,0:T(8,128)(2,1)} copy(bf16[256,16,128]{2,0,1:T(8,128)(2,1)S(1)} %bitcast.10) | data formatting | bytes 2097152
  39.4 1.6 %copy.11 = bf16[256,16,128]{2,1,0:T(8,128)(2,1)} copy(bf16[256,16,128]{2,0,1:T(8,128)(2,1)S(1)} %bitcast.9) | data formatting | bytes 2097152
Async XLA Ops:
  0.6 1.1 %copy-start.1 = (bf16[16,128,64]{1,2,0:T(8,128)(2,1)S(1)}, bf16[16,128,64]{1,2,0:T(8,128)(2,1)}, u32[]{:S(2)}) copy-start(bf16[16,128,64]{1,2,0:T(8,128)(2,1)} %param.8) | copy-start | bytes 786436
  0.6 1.1 %copy-start.2 = (bf16[2,128,64]{1,2,0:T(8,128)(2,1)S(1)}, bf16[2,128,64]{1,2,0:T(8,128)(2,1)}, u32[]{:S(2)}) copy-start(bf16[2,128,64]{1,2,0:T(8,128)(2,1)} %param.9) | copy-start | bytes 98308
  1.7 1.2 %copy-start = (bf16[256,16,128]{2,1,0:T(8,128)(2,1)S(1)}, bf16[256,16,128]{2,1,0:T(8,128)(2,1)}, u32[]{:S(2)}) copy-start(bf16[256,16,128]{2,1,0:T(8,128)(2,1)} %q_hbm.1) | copy-start | bytes 3145732

commit v4 on v3

--- a/solution.py
+++ b/solution.py
@@ -356,7 +356,7 @@
             dma((m,)),
         ],
         compiler_params=pltpu.CompilerParams(
-            collective_id=0, has_side_effects=True, vmem_limit_bytes=48 * 2**20
+            collective_id=0, has_side_effects=True, vmem_limit_bytes=61 * 2**20
         ),
     )(
         queries,

time: 43 us -> 44.5 us (1.035)
  Pallas kernels: 34.8 us -> 36.9 us
  local copies, waits for them, and re-layouts: 5.58 us -> 5 us
    pallas_call x1, Pallas kernels: 34.8 us -> 36.9 us  [local(): pl.pallas_call(functools.partial(kernel, n, m, count), out_shape=(pltpu.V...]
    unnamed x8 -> x2, local copies, waits for them, and re-layouts: 4.53 us -> 3.3 us
    transpose x1, local copies, waits for them, and re-layouts: 1.04 us -> 1.7 us  [local(): values.transpose(1, 0, 2)]
where the time goes in v4:
time: 44.5 us; the launch traced here: 44.3 us
  Pallas kernels  36.9 us (83%)
  local copies, waits for them, and re-layouts  5 us (11%)
  between operations  2.4 us (5%)
    pallas_call x1, Pallas kernels, local(): pl.pallas_call(functools.partial(kernel, n, m, count), out_shape=(pltpu.V...  36.9 us
    unnamed x2, local copies, waits for them, and re-layouts  3.3 us
    transpose x1, local copies, waits for them, and re-layouts, local(): values.transpose(1, 0, 2)  1.7 us

profile of v4, /device:TPU:0, one launch (start us, length us, event | category | flops | bytes accessed | tf_op | source)
XLA Modules:
  0.0 44.3 jit_solution(15909617314932339604)
XLA Ops:
  0.6 1.7 %copy_bitcast_fusion = (bf16[2,256,128]{2,1,0:T(8,128)(2,1)}, bf16[2,256,128]{2,1,0:T(8,128)(2,1)}) fusion(bf16[256,2,128]{2,1,0:T(2,128)(2,1)} %param.7, bf16[256,2,128]{2,1,0:T(2,128)(2,1)} %param.6), kind=kLoop, calls=%fused_computation | loop fusion | bytes 524288 | tf_op jit(solution)/shard_map/transpose | solution.py:364
  2.3 36.9 %shard_map.76 = (bf16[16,256,128]{2,1,0:T(8,128)(2,1)S(1)}, bf16[16,256,128]{2,1,0:T(8,128)(2,1)S(1)}, f32[1,1]{1,0:T(1,128)}) custom-call(bf16[256,16,128]{2,1,0:T(8,128)(2,1)} %q_hbm.1, bf16[2,256,128]{2,1,0:T(8,128)(2,1)} %get-tuple-element.13.k_ref, bf16[2,256,128]{2,1,0:T(8,128)(2,1)} %get-tuple-element.12.v_ref, bf16[16,64,128]{2,1,0:T(8,128)(2,1)} %bitcast.11, ...), custom_call_target="tpu_custom_call" | custom-call | tf_op jit(solution)/shard_map/pallas_call | solution.py:327
  39.2 1.6 %copy.10 = bf16[256,16,128]{2,1,0:T(8,128)(2,1)} copy(bf16[256,16,128]{2,0,1:T(8,128)(2,1)S(1)} %bitcast.10) | data formatting | bytes 2097152
  40.9 1.6 %copy.11 = bf16[256,16,128]{2,1,0:T(8,128)(2,1)} copy(bf16[256,16,128]{2,0,1:T(8,128)(2,1)S(1)} %bitcast.9) | data formatting | bytes 2097152
